TPU v7x, 32 devices: a whole 2x2x4 slice. The times are simulated.
32 devices in a mesh: tile: 8 (over z, x), mode: 4 (over y, core).
Axes of the slice: x: 2, y: 2, z: 4, core: 2. Of those that a mesh axis runs over, the one named last changes fastest.
Arguments:
- object_real: float32 [8, 2, 384, 384], P('tile', None, 'mode'), may hold values from 0.6 to 1.2
- object_imag: float32 [8, 2, 384, 384], P('tile', None, 'mode'), may hold values from -0.4 to 0.4
- probe: float32 [2, 8, 256, 256], P(None, 'mode'), may hold values from -1.5 to 1.5
- measured: float32 [8, 2, 256, 256], P('tile'), may hold values from 0.2 to 1.6
- positions: int32 [8, 2, 2], P('tile'), may hold values from 0 to 128
Outputs:
- object_grad_real: float32 [8, 2, 384, 384], P('tile', None, 'mode')
- object_grad_imag: float32 [8, 2, 384, 384], P('tile', None, 'mode')
- probe_grad: float32 [2, 8, 256, 256], P(None, 'mode')
All inputs are finite; a program needn't handle non-finite values.
Results may differ from a plain program's by a relative error of at most 0.0003.
Values sent between devices are 32-bit elements; how exact they have to be, the bound alone decides.
No kernel may reach another device: no remote copies, remote signals or barrier semaphores. Data moves between devices by JAX's collectives and lax.ppermute only.
A program may use at most 128 MiB of HBM per device.

v0:
```python
import functools
import math

import jax
import jax.numpy as jnp
from jax import lax
from jax.sharding import PartitionSpec as P

MARGIN = 64


amplitude_floor = 0.1
fresnel_number = 40.0


def padded(shard, sides, width):
    for axis, dim in sides:
        count, length = (lax.axis_size(axis), shard.shape[dim])
        up = [(i, (i + 1) % count) for i in range(count - 1)]
        down = [(j, i) for i, j in up]
        last = lax.slice_in_dim(shard, length - width, length, axis=dim)
        initial = lax.slice_in_dim(shard, 0, width, axis=dim)
        before = lax.ppermute(last, axis, up)
        after = lax.ppermute(initial, axis, down)
        shard = jnp.concatenate([before, shard, after], axis=dim)
    return shard


def tables(width):
    index = jnp.arange(width, dtype=jnp.int32)
    product = index[:, None] * index[None, :] % width
    angle = product.astype(jnp.float32) * (-2.0 * math.pi / width)
    scaling = 1.0 / math.sqrt(width)
    freq = ((index + width // 2) % width - width // 2).astype(jnp.float32) / width
    phase = -math.pi * fresnel_number * (freq[:, None] ** 2 + freq[None, :] ** 2)
    return (jnp.cos(angle) * scaling, jnp.sin(angle) * scaling, jnp.cos(phase), jnp.sin(phase))


def transform(real_part, imag_part, cos_table, sin_table):
    highest = lax.Precision.HIGHEST
    left_re = jnp.einsum("jk,mkl->mjl", cos_table, real_part, precision=highest) - jnp.einsum(
        "jk,mkl->mjl", sin_table, imag_part, precision=highest
    )
    left_im = jnp.einsum("jk,mkl->mjl", cos_table, imag_part, precision=highest) + jnp.einsum(
        "jk,mkl->mjl", sin_table, real_part, precision=highest
    )
    out_re = jnp.einsum("mjk,kl->mjl", left_re, cos_table, precision=highest) - jnp.einsum(
        "mjk,kl->mjl", left_im, sin_table, precision=highest
    )
    out_im = jnp.einsum("mjk,kl->mjl", left_re, sin_table, precision=highest) + jnp.einsum(
        "mjk,kl->mjl", left_im, cos_table, precision=highest
    )
    return (out_re, out_im)


def forward(cos_table, sin_table, kernel_re, kernel_im, crop_re, crop_im, probe_re, probe_im):
    wave_re, wave_im = (probe_re, probe_im)
    slices = crop_re.shape[0]
    for layer in range(slices):
        trans_re, trans_im = (crop_re[layer], crop_im[layer])
        wave_re, wave_im = (
            wave_re * trans_re - wave_im * trans_im,
            wave_re * trans_im + wave_im * trans_re,
        )
        if layer + 1 < slices:
            spec_re, spec_im = transform(wave_re, wave_im, cos_table, sin_table)
            spec_re, spec_im = (
                spec_re * kernel_re - spec_im * kernel_im,
                spec_re * kernel_im + spec_im * kernel_re,
            )
            wave_re, wave_im = transform(spec_re, spec_im, cos_table, -sin_table)
    return transform(wave_re, wave_im, cos_table, sin_table)


def add_window(target, update, start):
    current = lax.dynamic_slice(target, start, update.shape)
    return lax.dynamic_update_slice(target, current + update, start)


def body(object_real, object_imag, probe, measured, positions):
    tile_re, tile_im = (
        lax.all_gather(object_real[0], "mode", axis=1, tiled=True),
        lax.all_gather(object_imag[0], "mode", axis=1, tiled=True),
    )
    width = probe.shape[2]
    frames = measured.shape[1]
    slices = tile_re.shape[0]
    cos_table, sin_table, kernel_re, kernel_im = tables(width)
    model = functools.partial(forward, cos_table, sin_table, kernel_re, kernel_im)
    zero_index = jnp.zeros((), jnp.int32)
    fields = []
    pullbacks = []
    starts = []
    for frame in range(frames):
        start = (zero_index, positions[0, frame, 0], positions[0, frame, 1])
        crop_re = lax.dynamic_slice(tile_re, start, (slices, width, width))
        crop_im = lax.dynamic_slice(tile_im, start, (slices, width, width))
        field, pullback = jax.vjp(model, crop_re, crop_im, probe[0], probe[1])
        fields.append(field)
        pullbacks.append(pullback)
        starts.append(start)
    local_sum = jnp.stack(
        [jnp.sum(field[0] * field[0] + field[1] * field[1], axis=0) for field in fields]
    )
    intensity = lax.psum(local_sum, "mode")
    weight = 1.0 - measured[0] / jnp.sqrt(intensity + amplitude_floor)
    grad_re = jnp.zeros_like(tile_re)
    grad_im = jnp.zeros_like(tile_im)
    share_re = None
    share_im = None
    probe_total = jnp.zeros_like(probe)
    for frame in range(frames):
        field = fields[frame]
        factor = 2.0 * weight[frame]
        crop_gre, crop_gim, probe_gre, probe_gim = pullbacks[frame](
            (factor * field[0], factor * field[1])
        )
        probe_total = probe_total + jnp.stack([probe_gre, probe_gim])
        grad_re = add_window(grad_re, crop_gre, starts[frame])
        grad_im = add_window(grad_im, crop_gim, starts[frame])
    share_re, share_im = (
        lax.psum_scatter(grad_re, "mode", scatter_dimension=1, tiled=True),
        lax.psum_scatter(grad_im, "mode", scatter_dimension=1, tiled=True),
    )
    stacked = jnp.stack([share_re, share_im])
    extended = padded(stacked, (("tile", 3),), MARGIN)
    inner = extended[..., MARGIN:-MARGIN]
    summed = (
        inner.at[..., :MARGIN]
        .add(extended[..., :MARGIN])
        .at[..., -MARGIN:]
        .add(extended[..., -MARGIN:])
    )
    probe_grad = lax.psum(probe_total, "tile")
    return (summed[0][None], summed[1][None], probe_grad)


def solution(mesh):
    placed = (
        P("tile", None, "mode", None),
        P("tile", None, "mode", None),
        P(None, "mode", None, None),
        P("tile", None, None, None),
        P("tile", None, None),
    )
    return jax.shard_map(
        body,
        mesh=mesh,
        in_specs=placed,
        out_specs=(
            P("tile", None, "mode", None),
            P("tile", None, "mode", None),
            P(None, "mode", None, None),
        ),
        check_vma=False,
    )
```

profile of v0, /device:TPU:8, one launch (start us, length us, event | category | flops | bytes accessed | tf_op | source)
XLA Modules:
  0.0 512.1 jit_solution(14995246097614534255)
XLA Ops:
  20.5 7.6 %all-gather.5.cloned.1.call-done = f32[1,2,384,384]{3,2,1,0:T(8,128)} async-done(((f32[1,2,96,384]{3,2,1,0:T(8,128)}), f32[1,2,384,384]{3,2,1,0:T(8,128)}) %all-gather.5.cloned.1.call-update) | async-done | bytes 1179664 | tf_op jit(solution)/shard_map/all_gather | solution.py:82
  30.0 17.2 %all-gather.7.cloned.1.call-done = f32[1,2,384,384]{3,2,1,0:T(8,128)} async-done(((f32[1,2,96,384]{3,2,1,0:T(8,128)}), f32[1,2,384,384]{3,2,1,0:T(8,128)}) %all-gather.7.cloned.1.call-update) | async-done | bytes 1179664 | tf_op jit(solution)/shard_map/all_gather | solution.py:83
  47.2 2.4 dynamic-slice_bitcast_fusion.6
  70.4 2.0 fusion.204
  79.8 2.7 fusion.198
  82.5 2.1 fusion.202
  86.5 2.6 fusion.200
  89.1 2.6 fusion.132
  97.9 2.2 fusion.193
  109.1 2.0 fusion.188
  122.3 2.1 fusion.177
  133.8 2.3 fusion.24
  138.8 2.7 add_reduce_fusion.1
  143.3 2.6 add_reduce_fusion
  147.0 33.4 %all-reduce.15.cloned.1.call-done = f32[2,256,256]{2,1,0:T(8,128)} async-done(((f32[2,256,256]{2,1,0:T(8,128)}), f32[2,256,256]{2,1,0:T(8,128)}) %all-reduce.15.cloned.1.call-update) | async-done | bytes 524304 | tf_op jit(solution)/shard_map/psum | solution.py:105
  193.2 2.9 multiply_reduce_fusion.6
  205.8 2.1 fusion.17
  229.6 2.9 multiply_reduce_fusion.4
  242.3 2.1 fusion.5
  263.6 4.7 add_bitcast_fusion.1
  273.6 7.9 %dynamic_update_slice.12 = f32[2,384,384]{2,1,0:T(8,128)S(1)} dynamic-update-slice(f32[2,384,384]{2,1,0:T(8,128)S(1)} %broadcast.193.clone.1, f32[2,256,256]{2,1,0:T(8,128)S(1)} %pad_add_fusion.1, s32[]{:T(128)} %constant.90.clone.1, s32[]{:T(128)S(6)} %select_n.269, s32[]{:T(128)S(6)} %select_n.270) | dynamic-update-slice | bytes 1048580 | tf_op jit(solution)/shard_map/dynamic_update_slice | solution.py:77
  285.8 7.7 %dynamic_update_slice.14 = f32[2,384,384]{2,1,0:T(8,128)S(1)} dynamic-update-slice(f32[2,384,384]{2,1,0:T(8,128)S(1)} %broadcast.193.clone, f32[2,256,256]{2,1,0:T(8,128)S(1)} %pad_add_fusion, s32[]{:T(128)} %constant.90.clone.1, s32[]{:T(128)S(6)} %select_n.269, s32[]{:T(128)S(6)} %select_n.270) | dynamic-update-slice | bytes 1048580 | tf_op jit(solution)/shard_map/dynamic_update_slice | solution.py:77
  295.1 5.3 %dynamic_update_slice.13 = f32[2,384,384]{2,1,0:T(8,128)S(1)} dynamic-update-slice(f32[2,384,384]{2,1,0:T(8,128)S(1)} %dynamic_update_slice.12, f32[2,256,256]{2,1,0:T(8,128)S(1)} %get-tuple-element.97, s32[]{:T(128)} %constant.90.clone.1, s32[]{:T(128)S(6)} %select_n.273, s32[]{:T(128)S(6)} %select_n.274) | dynamic-update-slice | bytes 1048580 | tf_op jit(solution)/shard_map/dynamic_update_slice | solution.py:77
  302.3 5.2 %dynamic_update_slice.15 = f32[2,384,384]{2,1,0:T(8,128)S(1)} dynamic-update-slice(f32[2,384,384]{2,1,0:T(8,128)S(1)} %dynamic_update_slice.14, f32[2,256,256]{2,1,0:T(8,128)S(1)} %get-tuple-element.96, s32[]{:T(128)} %constant.90.clone.1, s32[]{:T(128)S(6)} %select_n.273, s32[]{:T(128)S(6)} %select_n.274) | dynamic-update-slice | bytes 1048580 | tf_op jit(solution)/shard_map/dynamic_update_slice | solution.py:77
  307.6 1.9 copy.279
  313.4 55.7 %all-reduce.19.cloned.1.call-done = (f32[2,384,384]{2,0,1:T(2,128)}, f32[2,384,384]{2,0,1:T(2,128)}) async-done(((f32[2,384,384]{2,0,1:T(2,128)}, f32[2,384,384]{2,0,1:T(2,128)}), (f32[2,384,384]{2,0,1:T(2,128)}, f32[2,384,384]{2,0,1:T(2,128)})) %all-reduce.19.cloned.1.call-update) | async-done | bytes 2359312
  371.5 3.4 collective-permute-start
  374.9 76.3 %all-reduce.17.cloned.1.call-done = f32[2,2,256,256]{2,3,1,0:T(8,128)} async-done(((f32[2,2,256,256]{2,3,1,0:T(8,128)}), f32[2,2,256,256]{2,3,1,0:T(8,128)}) %all-reduce.17.cloned.1.call-update) | async-done | bytes 1048592 | tf_op jit(solution)/shard_map/psum | solution.py:134
  451.2 2.5 copy.282
  453.9 3.5 collective-permute-start.1
  457.7 10.8 %scatter-add.6 = f32[2,2,96,384]{3,1,2,0:T(2,128)S(1)} dynamic-update-slice(f32[2,2,96,384]{3,1,2,0:T(2,128)S(1)} %pad_maximum_fusion, f32[2,2,96,64]{3,1,2,0:T(2,128)S(1)} %get-tuple-element.54, s32[]{:T(128)} %constant.90.clone.1, s32[]{:T(128)} %constant.90.clone.1, s32[]{:T(128)} %constant.90.clone.1, s32[]{:T(128)} %constant.90.clone.1) | dynamic-update-slice | bytes 196612 | tf_op jit(solution)/shard_map/scatter-add | solution.py:130
  468.7 34.9 %scatter-add.9 = f32[2,2,96,384]{3,1,2,0:T(2,128)S(1)} dynamic-update-slice(f32[2,2,96,384]{3,1,2,0:T(2,128)S(1)} %scatter-add.6, f32[2,2,96,64]{3,1,2,0:T(2,128)S(1)} %slice_add_fusion, s32[]{:T(128)} %constant.90.clone.1, s32[]{:T(128)} %constant.90.clone.1, s32[]{:T(128)} %constant.90.clone.1, s32[]{:T(128)} %constant.103.clone.1) | dynamic-update-slice | bytes 196612 | tf_op jit(solution)/shard_map/scatter-add | solution.py:132
  (213 shorter events, 171.8 us)
Async XLA Ops:
  7.2 21.0 %all-gather.5.cloned.1.call-start = ((), (), s32[]{:S(2)}) async-start(), calls=%async_computation.2 | async-start | bytes 1474560 | tf_op jit(solution)/shard_map/all_gather | solution.py:82
  7.9 39.3 %all-gather.7.cloned.1.call-start = ((), (), s32[]{:S(2)}) async-start(), calls=%async_computation.3 | async-start | bytes 1474560 | tf_op jit(solution)/shard_map/all_gather | solution.py:83
  8.6 171.8 %all-reduce.15.cloned.1.call-start = ((), (), s32[]{:S(2)}) async-start(), calls=%async_computation | async-start | bytes 1048576 | tf_op jit(solution)/shard_map/psum | solution.py:105
  50.7 8.5 %copy-start.8 = (f32[256,256]{0,1:T(8,128)}, f32[256,256]{0,1:T(8,128)S(1)}, u32[]{:S(2)}) copy-start(f32[256,256]{0,1:T(8,128)S(1)} %copy.187) | copy-start | bytes 786436
  78.0 6.6 %copy-start.2 = (f32[2,256,256]{2,1,0:T(8,128)}, f32[2,256,256]{2,1,0:T(8,128)S(1)}, u32[]{:S(2)}) copy-start(f32[2,256,256]{2,1,0:T(8,128)S(1)} %convolution_subtract_fusion.8) | copy-start | bytes 1572868
  79.8 4.8 copy-start.5
  91.9 10.0 %copy-start.10 = (f32[256,256]{0,1:T(8,128)}, f32[256,256]{0,1:T(8,128)S(1)}, u32[]{:S(2)}) copy-start(f32[256,256]{0,1:T(8,128)S(1)} %copy.208) | copy-start | bytes 786436
  93.1 8.9 %copy-start.12 = (f32[256,256]{0,1:T(8,128)}, f32[256,256]{0,1:T(8,128)S(1)}, u32[]{:S(2)}) copy-start(f32[256,256]{0,1:T(8,128)S(1)} %copy.209) | copy-start | bytes 786436
  122.3 11.5 %copy-start = (f32[2,256,256]{2,1,0:T(8,128)}, f32[2,256,256]{2,1,0:T(8,128)S(1)}, u32[]{:S(2)}) copy-start(f32[2,256,256]{2,1,0:T(8,128)S(1)} %convolution_add_fusion.26) | copy-start | bytes 1572868
  128.2 3.7 copy-start.3
  128.2 3.7 copy-start.6
  128.2 3.7 copy-start.22
  133.8 2.3 copy-start.32
  136.1 2.7 copy-start.34
  143.3 2.7 copy-start.14
  146.8 222.4 %all-reduce.19.cloned.1.call-start = ((), (), s32[]{:S(2)}) async-start(), calls=%async_computation.4 | async-start | bytes 4718592
  181.8 3.2 copy-start.17
  214.4 3.7 copy-start.33
  218.1 3.3 copy-start.15
  261.6 1.9 copy-start.9
  261.7 1.9 copy-start.11
  261.7 1.9 copy-start.13
  273.4 8.1 %copy-start.29 = (f32[256,256]{1,0:T(8,128)S(1)}, f32[256,256]{1,0:T(8,128)}, u32[]{:S(2)}) copy-start(f32[256,256]{1,0:T(8,128)} %get-tuple-element.36) | copy-start | bytes 786436
  273.5 8.1 %copy-start.30 = (f32[256,256]{1,0:T(8,128)S(1)}, f32[256,256]{1,0:T(8,128)}, u32[]{:S(2)}) copy-start(f32[256,256]{1,0:T(8,128)} %get-tuple-element.38) | copy-start | bytes 786436
  273.6 10.6 %copy-start.27 = (f32[256,256]{1,0:T(8,128)S(1)}, f32[256,256]{1,0:T(8,128)}, u32[]{:S(2)}) copy-start(f32[256,256]{1,0:T(8,128)} %get-tuple-element.37) | copy-start | bytes 786436
  273.6 10.6 %copy-start.28 = (f32[256,256]{1,0:T(8,128)S(1)}, f32[256,256]{1,0:T(8,128)}, u32[]{:S(2)}) copy-start(f32[256,256]{1,0:T(8,128)} %get-tuple-element.39) | copy-start | bytes 786436
  281.5 3.3 copy-start.31
  282.3 3.3 copy-start.23
  282.3 3.3 copy-start.24
  309.5 141.6 %all-reduce.17.cloned.1.call-start = ((), (), s32[]{:S(2)}) async-start(), calls=%async_computation.1 | async-start | bytes 2097152 | tf_op jit(solution)/shard_map/psum | solution.py:134
  371.5 82.2 %collective-permute-start = (f32[2,2,96,64]{3,1,2,0:T(2,128)S(1)}, f32[2,2,96,64]{3,1,2,0:T(2,128)S(1)}, u32[]{:S(2)}, u32[]{:S(2)}) collective-permute-start(f32[2,2,96,64]{3,1,2,0:T(2,128)S(1)} %fusion.232), channel_id=1, source_target_pairs={{0,4},{4,8},{8,12},{12,16},{16,20},{20,24},{24,28},{1,5},{5,9},{9,... | collective-permute-start | bytes 294920 | tf_op jit(solution)/shard_map/ppermute | solution.py:23
  453.9 14.6 %collective-permute-start.1 = (f32[2,2,96,64]{3,1,2,0:T(2,128)S(1)}, f32[2,2,96,64]{3,1,2,0:T(2,128)S(1)}, u32[]{:S(2)}, u32[]{:S(2)}) collective-permute-start(f32[2,2,96,64]{3,1,2,0:T(2,128)S(1)} %get-tuple-element.55), channel_id=1, source_target_pairs={{4,0},{8,4},{12,8},{16,12},{20,16},{24,20},{28,24},{5,1},{9,5},{13... | collective-permute-start | bytes 294920 | tf_op jit(solution)/shard_map/ppermute | solution.py:24
  (12 other events, 16.0 us)
Sparse Core Ops, SparseCore 0:
  9.5 18.5 all-gather.4
  29.7 17.4 all-gather.6
  146.9 33.4 all-reduce.14
  309.7 59.4 all-reduce.18
  373.1 78.0 all-reduce.16
where the time goes:
time: 521 us; the launch traced here: 512 us
  waiting for transfers between devices  192 us (37%)
  matrix products  178 us (34%)
  local copies, waits for them, and re-layouts  99.8 us (19%)
  between operations  23.8 us (5%)
  other arithmetic  11 us (2%)
  starting transfers between devices  7.24 us (1%)
    psum x1, waiting for transfers between devices, body(): probe_grad = lax.psum(probe_total, 'tile')  76.3 us
    unnamed x6, waiting for transfers between devices  57.2 us
    scatter-add x2, local copies, waits for them, and re-layouts, body(): summed = inner.at[..., :MARGIN].add(extended[..., :MARGIN]).at[..., -MARG...  45.7 us
    psum x1, waiting for transfers between devices, body(): intensity = lax.psum(local_sum, 'mode')  33.4 us
    dynamic_update_slice x6, local copies, waits for them, and re-layouts, add_window(): return lax.dynamic_update_slice(target, current + update, start)  30.1 us
    dot_general x12, matrix products, transform(): jnp.einsum('jk,mkl->mjl', cos_table, real_part, precision=highest)  26.6 us
    dot_general x12, matrix products, transform(): jnp.einsum('mjk,kl->mjl', left_im, cos_table, precision=highest)  22.1 us
    dot_general x12, matrix products, transform(): jnp.einsum('mjk,kl->mjl', left_re, cos_table, precision=highest)  22 us
  transfers between devices with their start and end apart: 7, of which 5 were waited for; matrix products, arithmetic and copies ran while one was open for 5% of the time, Pallas kernels for 0%

commit v1 on v0

v1 whole, which is shorter than its diff:
```python
import functools
import math

import jax
import jax.numpy as jnp
import numpy as np
from jax import lax
from jax.experimental import pallas as pl
from jax.experimental.pallas import tpu as pltpu
from jax.sharding import PartitionSpec as P

MARGIN = 64


amplitude_floor = 0.1
fresnel_number = 40.0

VM = pl.BlockSpec(memory_space=pltpu.VMEM)
SM = pl.BlockSpec(memory_space=pltpu.SMEM)
F32 = jnp.float32
BF16 = jnp.bfloat16


def real_form(w):
    return np.block([[w.real, w.imag], [-w.imag, w.real]])


def split_np(stack):
    full = np.stack(stack).astype(np.float32)
    hi = full.astype(BF16)
    lo = (full - hi.astype(np.float32)).astype(BF16)
    return np.stack([hi, lo], axis=1)


def make_tables(width):
    half = width // 2
    k = np.arange(width)
    root = np.exp(-2j * np.pi * (np.outer(k, k) % width) / width) / math.sqrt(width)
    even, odd = root[:half, 0::2], root[:half, 1::2]
    freq = ((k + half) % width - half) / width
    line = np.exp(-1j * np.pi * fresnel_number * freq**2)
    move = root.conj() @ (line[:, None] * root)
    plus = (move[:half, :half] + move[:half, half:]) / 2
    minus = (move[:half, :half] - move[:half, half:]) / 2
    dft = [real_form(even), real_form(odd)]
    prop = [real_form(plus), real_form(minus)]
    dft += [a.T for a in dft]
    prop += [a.T for a in prop]
    return split_np(dft), split_np(prop)


def split(x):
    hi = x.astype(BF16)
    return hi, (x - hi.astype(F32)).astype(BF16)


def mul_right(x, tab):
    hi, lo = split(x)
    lhs = jnp.concatenate([hi, lo, hi], axis=1)
    rhs = jnp.concatenate([tab[0], tab[0], tab[1]], axis=0)
    return jnp.dot(lhs, rhs, preferred_element_type=F32)


def mul_left(x, tab):
    hi, lo = split(x)
    lhs = jnp.concatenate([tab[0], tab[0], tab[1]], axis=1)
    rhs = jnp.concatenate([hi, lo, hi], axis=0)
    return jnp.dot(lhs, rhs, preferred_element_type=F32)


def along(x, axis, tabs, pre, post):
    half = x[0].shape[axis] // 2
    lo = [lax.slice_in_dim(p, 0, half, axis=axis) for p in x]
    up = [lax.slice_in_dim(p, half, 2 * half, axis=axis) for p in x]
    if pre:
        lo, up = [a + b for a, b in zip(lo, up)], [a - b for a, b in zip(lo, up)]
    mul = mul_right if axis == 1 else mul_left
    one = mul(jnp.concatenate(lo, axis=axis), tabs[0])
    two = mul(jnp.concatenate(up, axis=axis), tabs[1])
    if post:
        one, two = one + two, one - two
    return tuple(
        jnp.concatenate(
            [lax.slice_in_dim(q, i * half, (i + 1) * half, axis=axis) for q in (one, two)],
            axis=axis,
        )
        for i in range(2)
    )


def planes(x, right, left, pre, post):
    return along(along(x, 1, right, pre, post), 0, left, pre, post)


def load_tabs(ref, order):
    return [(ref[i, 0], ref[i, 1]) for i in order]


def times(a, b):
    return (a[0] * b[0] - a[1] * b[1], a[0] * b[1] + a[1] * b[0])


def conj_times(a, b):
    return (a[0] * b[0] + a[1] * b[1], a[0] * b[1] - a[1] * b[0])


def crop(pieces, where, tile, out):
    rows = pieces[0].shape[1]
    width = out.shape[1]
    for i, piece in enumerate(pieces):
        start = pl.multiple_of(where[2 + i] * rows, 8)
        for part in range(2):
            tile[part, pl.ds(start, rows), :] = piece[part]
    size = tile.shape[1]
    for part in range(2):
        x = pltpu.roll(tile[part], size - where[0], 0)[:width]
        out[part] = pltpu.roll(x, size - where[1], 1)[:, :width]


def spread(grad, where, tile, keep, send, frames):
    width = grad[0].shape[0]
    size = tile.shape[1]
    rows = keep.shape[2]
    for part in range(2):
        x = jnp.concatenate([grad[part], jnp.zeros((width, size - width), F32)], axis=1)
        x = pltpu.roll(x, where[1], 1)
        x = jnp.concatenate([x, jnp.zeros((size - width, size), F32)], axis=0)
        tile[part] = pltpu.roll(x, where[0], 0)
    for k in range(keep.shape[0]):
        for target, owner in ((keep, where[2 + frames * k]), (send, where[3 + frames * k])):
            start = pl.multiple_of(owner * rows, 8)
            for part in range(2):
                target[k, part] = tile[part, pl.ds(start, rows), :]


def sort_kernel(frame_ref, measured_ref, out_ref):
    width = out_ref.shape[0]
    half = width // 2
    i = lax.broadcasted_iota(jnp.int32, (width, width), 0)
    j = lax.broadcasted_iota(jnp.int32, (width, width), 1)
    pick = (j == jnp.where(i < half, 2 * i, 2 * (i - half) + 1)).astype(F32).astype(BF16)
    kcip = (i == jnp.where(j < half, 2 * j, 2 * (j - half) + 1)).astype(F32).astype(BF16)

    def three(x):
        hi = x.astype(BF16)
        rest = x - hi.astype(F32)
        mid = rest.astype(BF16)
        return [hi, mid, (rest - mid.astype(F32)).astype(BF16)]

    x = measured_ref[0, frame_ref[0]]
    x = jnp.dot(
        jnp.concatenate([pick] * 3, axis=1),
        jnp.concatenate(three(x), axis=0),
        preferred_element_type=F32,
    )
    out_ref[...] = jnp.dot(
        jnp.concatenate(three(x), axis=1),
        jnp.concatenate([kcip] * 3, axis=0),
        preferred_element_type=F32,
    )


def first_kernel(count, where, *refs):
    pieces = refs[:count]
    own, peer, tabs, wave, crop_ref, tile = refs[count:]
    crop(pieces, where, tile, crop_ref)
    obj = (crop_ref[0], crop_ref[1])
    right, left = load_tabs(tabs, (0, 1)), load_tabs(tabs, (2, 3))
    n = own.shape[1]
    for mode in range(2 * n):
        src = own if mode < n else peer
        x = times((src[0, mode % n], src[1, mode % n]), obj)
        wave[mode, 0], wave[mode, 1] = planes(x, right, left, True, True)


def second_kernel(count, where, *refs):
    pieces = refs[:count]
    wave, tabs, far, local, crop_ref, tile = refs[count:]
    crop(pieces, where, tile, crop_ref)
    obj = (crop_ref[0], crop_ref[1])
    right, left = load_tabs(tabs, (0, 1)), load_tabs(tabs, (2, 3))
    for mode in range(wave.shape[0]):
        x = times((wave[mode, 0], wave[mode, 1]), obj)
        re, im = planes(x, right, left, True, False)
        far[mode, 0], far[mode, 1] = re, im
        power = re * re + im * im
        local[...] = power if mode == 0 else local[...] + power


def third_kernel(frames, where, mine, other, measured, far, wave, crop_ref, tabs, back, keep, send, tile, acc):
    intensity = mine[...] + other[...]
    factor = 2.0 * (1.0 - measured[...] / jnp.sqrt(intensity + amplitude_floor))
    mine_obj = (crop_ref[0], crop_ref[1])
    right, left = load_tabs(tabs, (2, 3)), load_tabs(tabs, (0, 1))
    for mode in range(far.shape[0]):
        x = (factor * far[mode, 0], factor * far[mode, 1])
        g = planes(x, right, left, False, True)
        grad = conj_times((wave[mode, 0], wave[mode, 1]), g)
        for part in range(2):
            acc[part] = grad[part] if mode == 0 else acc[part] + grad[part]
        back[mode, 0], back[mode, 1] = conj_times(mine_obj, g)
    spread((acc[0], acc[1]), where, tile, keep, send, frames)


def fourth_kernel(frames, where, back, own, peer, crop_ref, tabs, pkeep, psend, keep, send, tile, acc):
    obj = (crop_ref[0], crop_ref[1])
    right, left = load_tabs(tabs, (2, 3)), load_tabs(tabs, (0, 1))
    n = own.shape[1]
    blocks, rows = pkeep.shape[0], pkeep.shape[3]
    for mode in range(2 * n):
        src, dst = (own, pkeep) if mode < n else (peer, psend)
        g = planes((back[mode, 0], back[mode, 1]), right, left, True, True)
        grad = conj_times((src[0, mode % n], src[1, mode % n]), g)
        for part in range(2):
            acc[part] = grad[part] if mode == 0 else acc[part] + grad[part]
        out = conj_times(obj, g)
        for part in range(2):
            for b in range(blocks):
                dst[b, part, mode % n] = out[part][b * rows : (b + 1) * rows]
    spread((acc[0], acc[1]), where, tile, keep, send, frames)


def call(kernel, outs, scratch, flops, *args):
    shapes = [jax.ShapeDtypeStruct(s, F32) for s in outs]
    moved = 4 * sum(math.prod(s) for s in outs) + 4 * sum(a.size for a in args)
    return pl.pallas_call(
        kernel,
        out_shape=shapes,
        in_specs=[SM] + [VM] * (len(args) - 1),
        out_specs=[VM] * len(shapes),
        scratch_shapes=[pltpu.VMEM(s, F32) for s in scratch],
        cost_estimate=pl.CostEstimate(flops=flops, bytes_accessed=moved, transcendentals=0),
        compiler_params=pltpu.CompilerParams(vmem_limit_bytes=56 * 2**20),
    )(*args)


def body(object_real, object_imag, probe, measured, positions):
    count = lax.axis_size("mode")
    tiles = lax.axis_size("tile")
    frames = measured.shape[1]
    cells = count // frames
    width = probe.shape[2]
    size = object_real.shape[3]
    rows = object_real.shape[2]
    slices = object_real.shape[1]
    modes = probe.shape[1]
    if frames != 2 or cells != 2 or slices != 2 or width % tiles:
        raise ValueError("unsupported split")
    dft_np, prop_np = make_tables(width)
    dft, prop = jnp.asarray(dft_np), jnp.asarray(prop_np)
    me = lax.axis_index("mode")
    frame, cell = me % frames, me // frames
    near = [(i, i ^ 1) for i in range(count)]
    far_away = [(i, i ^ frames) for i in range(count)]
    owners = [me, me ^ 1, me ^ frames, me ^ frames ^ 1]
    place = positions[0, frame].astype(jnp.int32)
    where = jnp.stack([place[0], place[1]] + [o.astype(jnp.int32) for o in owners])

    shards = [jnp.stack([object_real[0, s], object_imag[0, s]]) for s in range(slices)]
    from_y = [lax.ppermute(x, "mode", far_away) for x in shards]
    probe_peer = lax.ppermute(probe, "mode", near)
    from_core = [lax.ppermute(x, "mode", near) for x in shards]
    from_diag = [lax.ppermute(x, "mode", near) for x in from_y]

    unit = 4 * 2 * modes * 3 * 2 * width**3 * 2
    field = (2 * modes, 2, width, width)
    tile_shape = (2, size, size)
    part = (2, width, width)
    share = (cells, 2, rows, size)
    (sorted_measured,) = call(
        sort_kernel, [(width, width)], [], unit // 16, frame.astype(jnp.int32)[None], measured
    )
    pieces = [[shards[s], from_core[s], from_y[s], from_diag[s]] for s in range(slices)]
    wave, crop0 = call(
        functools.partial(first_kernel, count),
        [field, part],
        [tile_shape],
        unit,
        where,
        *pieces[0],
        probe,
        probe_peer,
        prop,
    )
    far, local, crop1 = call(
        functools.partial(second_kernel, count),
        [field, (width, width), part],
        [tile_shape],
        unit,
        where,
        *pieces[1],
        wave,
        dft,
    )
    other = lax.ppermute(local, "mode", far_away)
    back, keep1, send1 = call(
        functools.partial(third_kernel, frames),
        [field, share, share],
        [tile_shape, part],
        unit,
        where,
        local,
        other,
        sorted_measured,
        far,
        wave,
        crop1,
        dft,
    )
    block = (tiles, 2, modes, width // tiles, width)
    got1 = lax.ppermute(send1, "mode", near)
    pkeep, psend, keep0, send0 = call(
        functools.partial(fourth_kernel, frames),
        [block, block, share, share],
        [tile_shape, part],
        unit,
        where,
        back,
        probe,
        probe_peer,
        crop0,
        prop,
    )
    pgot = lax.ppermute(psend, "mode", near)
    got0 = lax.ppermute(send0, "mode", near)
    sums = [keep0 + got0, keep1 + got1]
    totals = [s[0] + lax.ppermute(s[1], "mode", far_away) for s in sums]
    pieces_in = lax.all_to_all(pkeep + pgot, "tile", 0, 0)
    mine = jnp.sum(pieces_in, axis=0)
    pieces_out = lax.all_to_all(jnp.broadcast_to(mine[None], block), "tile", 0, 0)
    probe_grad = jnp.transpose(pieces_out, (1, 2, 0, 3, 4)).reshape(probe.shape)

    total = jnp.stack(totals, axis=1)
    up = [(i, i + 1) for i in range(tiles - 1)]
    down = [(j, i) for i, j in up]
    before = lax.ppermute(total[..., -MARGIN:], "tile", up)
    after = lax.ppermute(total[..., :MARGIN], "tile", down)
    pad = [(0, 0)] * 3
    grads = (
        total
        + jnp.pad(before, pad + [(0, size - MARGIN)])
        + jnp.pad(after, pad + [(size - MARGIN, 0)])
    )
    return (grads[0][None], grads[1][None], probe_grad)


def solution(mesh):
    placed = (
        P("tile", None, "mode", None),
        P("tile", None, "mode", None),
        P(None, "mode", None, None),
        P("tile", None, None, None),
        P("tile", None, None),
    )
    return jax.shard_map(
        body,
        mesh=mesh,
        in_specs=placed,
        out_specs=(
            P("tile", None, "mode", None),
            P("tile", None, "mode", None),
            P(None, "mode", None, None),
        ),
        check_vma=False,
    )
```

time: 521 us -> 134 us (0.26); the launches traced: 512 us -> 133 us
  matrix products: 178 us -> 0 us
  waiting for transfers between devices: 192 us -> 61.5 us
  local copies, waits for them, and re-layouts: 99.8 us -> 10 us
  Pallas kernels: 0 us -> 31.3 us
  between operations: 23.8 us -> 0.85 us
  starting transfers between devices: 7.24 us -> 26.1 us
  other arithmetic: 11 us -> 2.88 us
    dot_general x96 -> x0, matrix products: 178 us -> none  [the longest x12 26.6 us: transform(): jnp.einsum('jk,mkl->mjl', cos_table, real_part, precision=highest)]
    psum x2 -> x0, waiting for transfers between devices: 110 us -> none  [the longest x1 76.3 us: body(): probe_grad = lax.psum(probe_total, 'tile')]
    unnamed x6 -> x0, waiting for transfers between devices: 57.2 us -> none
    scatter-add x2 -> x0, local copies, waits for them, and re-layouts: 45.7 us -> none  [body(): summed = inner.at[..., :MARGIN].add(extended[..., :MARGIN]).at[..., -MARG...]
    ppermute x2 -> x15, waiting for transfers between devices: 0.01 us -> 38.4 us  [the longest x2 12.5 us: body(): totals = [s[0] + lax.ppermute(s[1], 'mode', far_away) for s in sums]]
    pallas_call x0 -> x5, Pallas kernels: none -> 31.3 us  [call(): pl.pallas_call(kernel, out_shape=shapes, in_specs=[SM] + [VM] * (len(args...]
    dynamic_update_slice x6 -> x0, local copies, waits for them, and re-layouts: 30.1 us -> none  [add_window(): return lax.dynamic_update_slice(target, current + update, start)]
    all_gather x2 -> x0, waiting for transfers between devices: 24.8 us -> none  [the longest x1 17.2 us: body(): lax.all_gather(object_imag[0], 'mode', axis=1, tiled=True)]
  transfers between devices with their start and end apart: 7 -> 17, of which waited for: 5 -> 9; matrix products, arithmetic and copies ran while one was open for 5% -> 5% of each run, Pallas kernels for 0% -> 7%
where the time goes in v1:
time: 134 us; the launch traced here: 133 us
  waiting for transfers between devices  61.5 us (46%)
  Pallas kernels  31.3 us (23%)
  starting transfers between devices  26.1 us (19%)
  local copies, waits for them, and re-layouts  10 us (7%)
  other arithmetic  2.88 us (2%)
    pallas_call x5, Pallas kernels, call(): pl.pallas_call(kernel, out_shape=shapes, in_specs=[SM] + [VM] * (len(args...  31.3 us
    all_to_all x1, waiting for transfers between devices, body(): pieces_in = lax.all_to_all(pkeep + pgot, 'tile', 0, 0)  23.1 us
    ppermute x2, waiting for transfers between devices, body(): totals = [s[0] + lax.ppermute(s[1], 'mode', far_away) for s in sums]  12.5 us
    ppermute x2, waiting for transfers between devices, body(): from_y = [lax.ppermute(x, 'mode', far_away) for x in shards]  10.5 us
    all_to_all x1, starting transfers between devices, body(): pieces_in = lax.all_to_all(pkeep + pgot, 'tile', 0, 0)  6.25 us
    all_to_all x1, starting transfers between devices, body(): lax.all_to_all(jnp.broadcast_to(mine[None], block), 'tile', 0, 0)  6.18 us
    ppermute x1, waiting for transfers between devices, body(): other = lax.ppermute(local, 'mode', far_away)  5.02 us
    unnamed x27, local copies, waits for them, and re-layouts  4.15 us
  transfers between devices with their start and end apart: 17, of which 9 were waited for; matrix products, arithmetic and copies ran while one was open for 5% of the time, Pallas kernels for 7%

profile of v1, /device:TPU:8, one launch (start us, length us, event | category | flops | bytes accessed | tf_op | source)
XLA Modules:
  0.0 132.7 jit_solution(6933654288242322008)
XLA Ops:
  0.7 1.2 slice_bitcast_fusion.6
  1.9 1.6 %collective-permute-start.4 = (f32[2,96,384]{2,1,0:T(8,128)S(1)}, f32[2,96,384]{2,1,0:T(8,128)S(1)}, u32[]{:S(2)}, u32[]{:S(2)}) collective-permute-start(f32[2,96,384]{2,1,0:T(8,128)S(1)} %pad_maximum_fusion.2.refs_0_), channel_id=1, source_target_pairs={{0,2},{1,3},{2,0},{3,1},{4,6},{5,7},{6,4},{7,5},{8,10},{9,11},{10,... | collective-permute-start | bytes 884744 | tf_op jit(solution)/shard_map/ppermute | solution.py:260
  4.1 7.8 %collective-permute-done.4.refs_2_ = f32[2,96,384]{2,1,0:T(8,128)S(1)} collective-permute-done((f32[2,96,384]{2,1,0:T(8,128)S(1)}, f32[2,96,384]{2,1,0:T(8,128)S(1)}, u32[]{:S(2)}, u32[]{:S(2)}) %collective-permute-start.4) | collective-permute-done | bytes 294944 | tf_op jit(solution)/shard_map/ppermute | solution.py:260
  12.4 0.6 fusion.8
  13.0 1.9 %stack.34.where = s32[6]{0:T(128)} concatenate(s32[1]{0:T(128)} %bitcast, s32[1]{0:T(128)} %bitcast.1, s32[1]{0:T(128)} %bitcast.2, s32[1]{0:T(128)} %bitcast.3, s32[1]{0:T(128)} %bitcast.4, s32[1]{0:T(128)} %bitcast.5), dimensions={0} | concatenate | bytes 48 | tf_op jit(solution)/shard_map/stack | solution.py:257
  14.9 2.8 %collective-permute-done.1.refs_2_ = f32[2,96,384]{2,1,0:T(8,128)S(1)} collective-permute-done((f32[2,96,384]{2,1,0:T(8,128)S(1)}, f32[2,96,384]{2,1,0:T(8,128)S(1)}, u32[]{:S(2)}, u32[]{:S(2)}) %collective-permute-start.1) | collective-permute-done | bytes 294944 | tf_op jit(solution)/shard_map/ppermute | solution.py:260
  17.8 0.7 copy-done.9
  18.6 1.0 copy-done.5
  19.6 6.7 %shard_map.94 = (f32[4,2,256,256]{3,2,1,0:T(8,128)}, f32[2,256,256]{2,1,0:T(8,128)}) custom-call(s32[6]{0:T(128)} %stack.34.where, f32[2,96,384]{2,1,0:T(8,128)} %copy-done.4, f32[2,96,384]{2,1,0:T(8,128)} %copy-done.9, f32[2,96,384]{2,1,0:T(8,128)} %copy-done.7, f32[2,96,384]{2,1,0:T(8,128)} %copy-done.10, f32[2,2,256,256]{3,2,1,0:T(8,128)} %own.1, ...), custom_call_target="tpu_custom_call" | custom-call | flops 3221225472 | bytes 7995416 | tf_op jit(solution)/shard_map/pallas_call | solution.py:226
  26.3 0.7 copy-done.8
  27.1 7.0 %shard_map.95 = (f32[4,2,256,256]{3,2,1,0:T(8,128)}, f32[256,256]{1,0:T(8,128)}, f32[2,256,256]{2,1,0:T(8,128)}) custom-call(s32[6]{0:T(128)} %stack.34.where, f32[2,96,384]{2,1,0:T(8,128)} %copy-done.3, f32[2,96,384]{2,1,0:T(8,128)} %copy-done.8, f32[2,96,384]{2,1,0:T(8,128)} %copy-done.6, f32[2,96,384]{2,1,0:T(8,128)} %copy-done.11, ...), custom_call_target="tpu_custom_call" | custom-call | flops 3221225472 | bytes 8257560 | tf_op jit(solution)/shard_map/pallas_call | solution.py:226
  34.1 1.5 %collective-permute-start.7 = (f32[256,256]{1,0:T(8,128)}, f32[256,256]{1,0:T(8,128)S(1)}, u32[]{:S(2)}, u32[]{:S(2)}) collective-permute-start(f32[256,256]{1,0:T(8,128)} %get-tuple-element.16.mine), channel_id=1, source_target_pairs={{0,2},{1,3},{2,0},{3,1},{4,6},{5,7},{6,4},{7,5},{8,10},{9,11},{10,... | collective-permute-start | bytes 786440 | tf_op jit(solution)/shard_map/ppermute | solution.py:295
  35.7 2.4 %shard_map.96.measured = f32[256,256]{1,0:T(8,128)} custom-call(s32[1]{0:T(128)} %bitcast.10.frame_ref, f32[1,2,256,256]{3,2,1,0:T(8,128)} %measured_ref.1), custom_call_target="tpu_custom_call" | custom-call | flops 201326592 | bytes 786436 | tf_op jit(solution)/shard_map/pallas_call | solution.py:226
  38.0 5.0 %collective-permute-done.7.other = f32[256,256]{1,0:T(8,128)S(1)} collective-permute-done((f32[256,256]{1,0:T(8,128)}, f32[256,256]{1,0:T(8,128)S(1)}, u32[]{:S(2)}, u32[]{:S(2)}) %collective-permute-start.7) | collective-permute-done | bytes 262176 | tf_op jit(solution)/shard_map/ppermute | solution.py:295
  43.1 0.7 copy-done.12
  43.8 7.6 %shard_map.97 = (f32[4,2,256,256]{3,2,1,0:T(8,128)}, f32[2,2,96,384]{3,2,1,0:T(8,128)}, f32[2,2,96,384]{3,2,1,0:T(8,128)}) custom-call(s32[6]{0:T(128)} %stack.34.where, f32[256,256]{1,0:T(8,128)} %get-tuple-element.16.mine, f32[256,256]{1,0:T(8,128)} %copy-done.12, f32[256,256]{1,0:T(8,128)} %shard_map.96.measured, ...), custom_call_target="tpu_custom_call" | custom-call | flops 3221225472 | bytes 10879000 | tf_op jit(solution)/shard_map/pallas_call | solution.py:226
  51.3 7.6 %shard_map.98 = (f32[8,2,2,32,256]{4,3,2,1,0:T(8,128)}, f32[8,2,2,32,256]{4,3,2,1,0:T(8,128)}, f32[2,2,96,384]{3,2,1,0:T(8,128)}, f32[2,2,96,384]{3,2,1,0:T(8,128)}) custom-call(s32[6]{0:T(128)} %stack.34.where, f32[4,2,256,256]{3,2,1,0:T(8,128)} %get-tuple-element.19.back, f32[2,2,256,256]{3,2,1,0:T(8,128)} %own.1, f32[2,2,256,256]{3,2,1,0:T(8,128)} %copy-done.5, ...), custom_call_target="tpu_custom_call" | custom-call | flops 3221225472 | bytes 10092568 | tf_op jit(solution)/shard_map/pallas_call | solution.py:226
  58.9 2.9 %collective-permute-done.14 = f32[8,2,2,32,256]{4,3,2,1,0:T(8,128)S(1)} collective-permute-done((f32[8,2,2,32,256]{4,3,2,1,0:T(8,128)}, f32[8,2,2,32,256]{4,3,2,1,0:T(8,128)S(1)}, u32[]{:S(2)}, u32[]{:S(2)}) %collective-permute-start.14) | collective-permute-done | bytes 1048608 | tf_op jit(solution)/shard_map/ppermute | solution.py:324
  61.8 2.3 %add.40 = f32[8,2,2,32,256]{4,3,2,1,0:T(8,128)} add(f32[8,2,2,32,256]{4,3,2,1,0:T(8,128)} %get-tuple-element.25, f32[8,2,2,32,256]{4,3,2,1,0:T(8,128)S(1)} %collective-permute-done.14) | non-fusion elementwise | flops 262144 | bytes 3145728 | tf_op jit(solution)/shard_map/add | solution.py:328
  64.1 6.3 %all-to-all-start = ((f32[8,2,2,32,256]{4,3,2,1,0:T(8,128)}), f32[8,2,2,32,256]{4,3,2,1,0:T(8,128)S(1)}, u32[]{:S(2)}, u32[]{:S(2)}) async-start(f32[8,2,2,32,256]{4,3,2,1,0:T(8,128)} %add.40), calls=%async_computation | async-start | bytes 2097152 | tf_op jit(solution)/shard_map/all_to_all | solution.py:328
  70.9 23.1 %all-to-all-done = f32[8,2,2,32,256]{4,3,2,1,0:T(8,128)S(1)} async-done(((f32[8,2,2,32,256]{4,3,2,1,0:T(8,128)}), f32[8,2,2,32,256]{4,3,2,1,0:T(8,128)S(1)}, u32[]{:S(2)}, u32[]{:S(2)}) %all-to-all-start) | async-done | bytes 1048608 | tf_op jit(solution)/shard_map/all_to_all | solution.py:328
  94.1 1.1 broadcast_in_dim.10
  95.2 6.2 %all-to-all-start.1 = ((f32[8,2,2,32,256]{4,3,2,1,0:T(8,128)}), f32[8,2,2,32,256]{4,3,2,1,0:T(8,128)S(1)}, u32[]{:S(2)}, u32[]{:S(2)}) async-start(f32[8,2,2,32,256]{4,3,2,1,0:T(8,128)} %broadcast_in_dim.10), calls=%async_computation.1 | async-start | bytes 2097152 | tf_op jit(solution)/shard_map/all_to_all | solution.py:330
  101.5 1.6 %collective-permute-start.9 = (f32[2,96,384]{2,1,0:T(8,128)S(1)}, f32[2,96,384]{2,1,0:T(8,128)S(1)}, u32[]{:S(2)}, u32[]{:S(2)}) collective-permute-start(f32[2,96,384]{2,1,0:T(8,128)S(1)} %slice_bitcast_fusion.4), channel_id=1, source_target_pairs={{0,2},{1,3},{2,0},{3,1},{4,6},{5,7},{6,4},{7,5},{8,10},{9,11},{10,... | collective-permute-start | bytes 884744 | tf_op jit(solution)/shard_map/ppermute | solution.py:327
  103.8 7.7 %collective-permute-done.9 = f32[2,96,384]{2,1,0:T(8,128)S(1)} collective-permute-done((f32[2,96,384]{2,1,0:T(8,128)S(1)}, f32[2,96,384]{2,1,0:T(8,128)S(1)}, u32[]{:S(2)}, u32[]{:S(2)}) %collective-permute-start.9) | collective-permute-done | bytes 294944 | tf_op jit(solution)/shard_map/ppermute | solution.py:327
  111.5 4.8 %collective-permute-done.11 = f32[2,96,384]{2,1,0:T(8,128)S(1)} collective-permute-done((f32[2,96,384]{2,1,0:T(8,128)S(1)}, f32[2,96,384]{2,1,0:T(8,128)S(1)}, u32[]{:S(2)}, u32[]{:S(2)}) %collective-permute-start.11) | collective-permute-done | bytes 294944 | tf_op jit(solution)/shard_map/ppermute | solution.py:327
  116.4 3.4 %collective-permute-start.12 = (f32[2,2,96,64]{3,2,0,1:T(8,128)S(1)}, f32[2,2,96,64]{3,2,0,1:T(8,128)S(1)}, u32[]{:S(2)}, u32[]{:S(2)}) collective-permute-start(f32[2,2,96,64]{3,2,0,1:T(8,128)S(1)} %get-tuple-element.38), channel_id=1, source_target_pairs={{0,4},{4,8},{8,12},{12,16},{16,20},{20,24},{24,28},{1,5},{5,9},{9,... | collective-permute-start | bytes 294920 | tf_op jit(solution)/shard_map/ppermute | solution.py:336
  119.8 3.4 %collective-permute-start.13 = (f32[2,2,96,64]{3,2,0,1:T(8,128)S(1)}, f32[2,2,96,64]{3,2,0,1:T(8,128)S(1)}, u32[]{:S(2)}, u32[]{:S(2)}) collective-permute-start(f32[2,2,96,64]{3,2,0,1:T(8,128)S(1)} %get-tuple-element.39), channel_id=1, source_target_pairs={{4,0},{8,4},{12,8},{16,12},{20,16},{24,20},{28,24},{5,1},{9,5},{13... | collective-permute-start | bytes 294920 | tf_op jit(solution)/shard_map/ppermute | solution.py:337
  123.2 3.4 %collective-permute-done.12 = f32[2,2,96,64]{3,2,0,1:T(8,128)S(1)} collective-permute-done((f32[2,2,96,64]{3,2,0,1:T(8,128)S(1)}, f32[2,2,96,64]{3,2,0,1:T(8,128)S(1)}, u32[]{:S(2)}, u32[]{:S(2)}) %collective-permute-start.12) | collective-permute-done | bytes 98336 | tf_op jit(solution)/shard_map/ppermute | solution.py:336
  126.5 4.1 %collective-permute-done.13 = f32[2,2,96,64]{3,2,0,1:T(8,128)S(1)} collective-permute-done((f32[2,2,96,64]{3,2,0,1:T(8,128)S(1)}, f32[2,2,96,64]{3,2,0,1:T(8,128)S(1)}, u32[]{:S(2)}, u32[]{:S(2)}) %collective-permute-start.13) | collective-permute-done | bytes 98336 | tf_op jit(solution)/shard_map/ppermute | solution.py:337
  130.8 0.9 slice_bitcast_fusion
  131.6 1.0 copy.14
  (52 shorter events, 3.1 us)
Async XLA Ops:
  0.6 11.8 %copy-start = (s32[1,2,2]{2,1,0:T(2,128)S(1)}, s32[1,2,2]{2,1,0:T(2,128)}, u32[]{:S(2)}) copy-start(s32[1,2,2]{2,1,0:T(2,128)} %param.11) | copy-start | bytes 52
  0.6 17.1 %collective-permute-start.6 = (f32[2,2,256,256]{3,2,1,0:T(8,128)}, f32[2,2,256,256]{3,2,1,0:T(8,128)S(1)}, u32[]{:S(2)}, u32[]{:S(2)}) collective-permute-start(f32[2,2,256,256]{3,2,1,0:T(8,128)} %own.1), channel_id=1, source_target_pairs={{0,1},{1,0},{2,3},{3,2},{4,5},{5,4},{6,7},{7,6},{8,9},{9,8},{10,11... | collective-permute-start | bytes 3145736 | tf_op jit(solution)/shard_map/ppermute | solution.py:261
  1.9 15.9 %copy-start.4 = (f32[2,96,384]{2,1,0:T(8,128)}, f32[2,96,384]{2,1,0:T(8,128)S(1)}, u32[]{:S(2)}) copy-start(f32[2,96,384]{2,1,0:T(8,128)S(1)} %pad_maximum_fusion.2.refs_0_) | copy-start | bytes 884740
  1.9 9.9 %collective-permute-start.4 = (f32[2,96,384]{2,1,0:T(8,128)S(1)}, f32[2,96,384]{2,1,0:T(8,128)S(1)}, u32[]{:S(2)}, u32[]{:S(2)}) collective-permute-start(f32[2,96,384]{2,1,0:T(8,128)S(1)} %pad_maximum_fusion.2.refs_0_), channel_id=1, source_target_pairs={{0,2},{1,3},{2,0},{3,1},{4,6},{5,7},{6,4},{7,5},{8,10},{9,11},{10,... | collective-permute-start | bytes 884744 | tf_op jit(solution)/shard_map/ppermute | solution.py:260
  3.5 22.7 %copy-start.3 = (f32[2,96,384]{2,1,0:T(8,128)}, f32[2,96,384]{2,1,0:T(8,128)S(1)}, u32[]{:S(2)}) copy-start(f32[2,96,384]{2,1,0:T(8,128)S(1)} %pad_maximum_fusion.1.refs_0_) | copy-start | bytes 884740
  3.6 14.2 %collective-permute-start.1 = (f32[2,96,384]{2,1,0:T(8,128)S(1)}, f32[2,96,384]{2,1,0:T(8,128)S(1)}, u32[]{:S(2)}, u32[]{:S(2)}) collective-permute-start(f32[2,96,384]{2,1,0:T(8,128)S(1)} %pad_maximum_fusion.1.refs_0_), channel_id=1, source_target_pairs={{0,2},{1,3},{2,0},{3,1},{4,6},{5,7},{6,4},{7,5},{8,10},{9,11},{10,... | collective-permute-start | bytes 884744 | tf_op jit(solution)/shard_map/ppermute | solution.py:260
  4.1 13.6 %collective-permute-start.3 = (f32[2,96,384]{2,1,0:T(8,128)S(1)}, f32[2,96,384]{2,1,0:T(8,128)S(1)}, u32[]{:S(2)}, u32[]{:S(2)}) collective-permute-start(f32[2,96,384]{2,1,0:T(8,128)S(1)} %pad_maximum_fusion.2.refs_0_), channel_id=1, source_target_pairs={{0,1},{1,0},{2,3},{3,2},{4,5},{5,4},{6,7},{7,6},{8,9},{9,8},{10,11... | collective-permute-start | bytes 884744 | tf_op jit(solution)/shard_map/ppermute | solution.py:262
  11.9 5.9 %copy-start.7 = (f32[2,96,384]{2,1,0:T(8,128)}, f32[2,96,384]{2,1,0:T(8,128)S(1)}, u32[]{:S(2)}) copy-start(f32[2,96,384]{2,1,0:T(8,128)S(1)} %collective-permute-done.4.refs_2_) | copy-start | bytes 884740
  11.9 5.9 %collective-permute-start.5 = (f32[2,96,384]{2,1,0:T(8,128)S(1)}, f32[2,96,384]{2,1,0:T(8,128)S(1)}, u32[]{:S(2)}, u32[]{:S(2)}) collective-permute-start(f32[2,96,384]{2,1,0:T(8,128)S(1)} %collective-permute-done.4.refs_2_), channel_id=1, source_target_pairs={{0,1},{1,0},{2,3},{3,2},{4,5},{5,4},{6,7},{7,6},{8,9},{9,8},{10,11... | collective-permute-start | bytes 884744 | tf_op jit(solution)/shard_map/ppermute | solution.py:263
  11.9 14.4 %collective-permute-start = (f32[2,96,384]{2,1,0:T(8,128)S(1)}, f32[2,96,384]{2,1,0:T(8,128)S(1)}, u32[]{:S(2)}, u32[]{:S(2)}) collective-permute-start(f32[2,96,384]{2,1,0:T(8,128)S(1)} %pad_maximum_fusion.1.refs_0_), channel_id=1, source_target_pairs={{0,1},{1,0},{2,3},{3,2},{4,5},{5,4},{6,7},{7,6},{8,9},{9,8},{10,11... | collective-permute-start | bytes 884744 | tf_op jit(solution)/shard_map/ppermute | solution.py:262
  17.7 8.6 %copy-start.6 = (f32[2,96,384]{2,1,0:T(8,128)}, f32[2,96,384]{2,1,0:T(8,128)S(1)}, u32[]{:S(2)}) copy-start(f32[2,96,384]{2,1,0:T(8,128)S(1)} %collective-permute-done.1.refs_2_) | copy-start | bytes 884740
  17.7 8.6 %collective-permute-start.2 = (f32[2,96,384]{2,1,0:T(8,128)S(1)}, f32[2,96,384]{2,1,0:T(8,128)S(1)}, u32[]{:S(2)}, u32[]{:S(2)}) collective-permute-start(f32[2,96,384]{2,1,0:T(8,128)S(1)} %collective-permute-done.1.refs_2_), channel_id=1, source_target_pairs={{0,1},{1,0},{2,3},{3,2},{4,5},{5,4},{6,7},{7,6},{8,9},{9,8},{10,11... | collective-permute-start | bytes 884744 | tf_op jit(solution)/shard_map/ppermute | solution.py:263
  17.7 0.8 copy-start.9
  17.8 0.8 copy-start.10
  18.6 1.0 copy-start.5
  26.3 0.7 copy-start.8
  26.3 0.8 copy-start.11
  34.1 8.9 %collective-permute-start.7 = (f32[256,256]{1,0:T(8,128)}, f32[256,256]{1,0:T(8,128)S(1)}, u32[]{:S(2)}, u32[]{:S(2)}) collective-permute-start(f32[256,256]{1,0:T(8,128)} %get-tuple-element.16.mine), channel_id=1, source_target_pairs={{0,2},{1,3},{2,0},{3,1},{4,6},{5,7},{6,4},{7,5},{8,10},{9,11},{10,... | collective-permute-start | bytes 786440 | tf_op jit(solution)/shard_map/ppermute | solution.py:295
  43.0 0.7 copy-start.12
  58.9 2.9 %collective-permute-start.14 = (f32[8,2,2,32,256]{4,3,2,1,0:T(8,128)}, f32[8,2,2,32,256]{4,3,2,1,0:T(8,128)S(1)}, u32[]{:S(2)}, u32[]{:S(2)}) collective-permute-start(f32[8,2,2,32,256]{4,3,2,1,0:T(8,128)} %get-tuple-element.26), channel_id=1, source_target_pairs={{0,1},{1,0},{2,3},{3,2},{4,5},{5,4},{6,7},{7,6},{8,9},{9,8},{10,11... | collective-permute-start | bytes 3145736 | tf_op jit(solution)/shard_map/ppermute | solution.py:324
  64.1 29.9 %all-to-all-start = ((f32[8,2,2,32,256]{4,3,2,1,0:T(8,128)}), f32[8,2,2,32,256]{4,3,2,1,0:T(8,128)S(1)}, u32[]{:S(2)}, u32[]{:S(2)}) async-start(f32[8,2,2,32,256]{4,3,2,1,0:T(8,128)} %add.40), calls=%async_computation | async-start | bytes 2097152 | tf_op jit(solution)/shard_map/all_to_all | solution.py:328
  70.4 31.0 %collective-permute-start.8 = (f32[2,2,96,384]{3,2,1,0:T(8,128)}, f32[2,2,96,384]{3,2,1,0:T(8,128)S(1)}, u32[]{:S(2)}, u32[]{:S(2)}) collective-permute-start(f32[2,2,96,384]{3,2,1,0:T(8,128)} %get-tuple-element.22), channel_id=1, source_target_pairs={{0,1},{1,0},{2,3},{3,2},{4,5},{5,4},{6,7},{7,6},{8,9},{9,8},{10,11... | collective-permute-start | bytes 1769480 | tf_op jit(solution)/shard_map/ppermute | solution.py:325
  70.4 31.0 %copy-start.2 = (f32[2,2,96,384]{3,2,1,0:T(8,128)S(1)}, f32[2,2,96,384]{3,2,1,0:T(8,128)}, u32[]{:S(2)}) copy-start(f32[2,2,96,384]{3,2,1,0:T(8,128)} %get-tuple-element.21) | copy-start | bytes 1769476
  70.4 32.7 %collective-permute-start.10 = (f32[2,2,96,384]{3,2,1,0:T(8,128)}, f32[2,2,96,384]{3,2,1,0:T(8,128)S(1)}, u32[]{:S(2)}, u32[]{:S(2)}) collective-permute-start(f32[2,2,96,384]{3,2,1,0:T(8,128)} %get-tuple-element.24), channel_id=1, source_target_pairs={{0,1},{1,0},{2,3},{3,2},{4,5},{5,4},{6,7},{7,6},{8,9},{9,8},{10,11... | collective-permute-start | bytes 1769480 | tf_op jit(solution)/shard_map/ppermute | solution.py:311
  95.2 7.9 %copy-start.1 = (f32[2,2,96,384]{3,2,1,0:T(8,128)S(1)}, f32[2,2,96,384]{3,2,1,0:T(8,128)}, u32[]{:S(2)}) copy-start(f32[2,2,96,384]{3,2,1,0:T(8,128)} %get-tuple-element.23) | copy-start | bytes 1769476
  95.2 36.4 %all-to-all-start.1 = ((f32[8,2,2,32,256]{4,3,2,1,0:T(8,128)}), f32[8,2,2,32,256]{4,3,2,1,0:T(8,128)S(1)}, u32[]{:S(2)}, u32[]{:S(2)}) async-start(f32[8,2,2,32,256]{4,3,2,1,0:T(8,128)} %broadcast_in_dim.10), calls=%async_computation.1 | async-start | bytes 2097152 | tf_op jit(solution)/shard_map/all_to_all | solution.py:330
  101.5 9.9 %collective-permute-start.9 = (f32[2,96,384]{2,1,0:T(8,128)S(1)}, f32[2,96,384]{2,1,0:T(8,128)S(1)}, u32[]{:S(2)}, u32[]{:S(2)}) collective-permute-start(f32[2,96,384]{2,1,0:T(8,128)S(1)} %slice_bitcast_fusion.4), channel_id=1, source_target_pairs={{0,2},{1,3},{2,0},{3,1},{4,6},{5,7},{6,4},{7,5},{8,10},{9,11},{10,... | collective-permute-start | bytes 884744 | tf_op jit(solution)/shard_map/ppermute | solution.py:327
  103.2 13.1 %collective-permute-start.11 = (f32[2,96,384]{2,1,0:T(8,128)S(1)}, f32[2,96,384]{2,1,0:T(8,128)S(1)}, u32[]{:S(2)}, u32[]{:S(2)}) collective-permute-start(f32[2,96,384]{2,1,0:T(8,128)S(1)} %slice_bitcast_fusion.2), channel_id=1, source_target_pairs={{0,2},{1,3},{2,0},{3,1},{4,6},{5,7},{6,4},{7,5},{8,10},{9,11},{10,... | collective-permute-start | bytes 884744 | tf_op jit(solution)/shard_map/ppermute | solution.py:327
  116.4 10.1 %collective-permute-start.12 = (f32[2,2,96,64]{3,2,0,1:T(8,128)S(1)}, f32[2,2,96,64]{3,2,0,1:T(8,128)S(1)}, u32[]{:S(2)}, u32[]{:S(2)}) collective-permute-start(f32[2,2,96,64]{3,2,0,1:T(8,128)S(1)} %get-tuple-element.38), channel_id=1, source_target_pairs={{0,4},{4,8},{8,12},{12,16},{16,20},{20,24},{24,28},{1,5},{5,9},{9,... | collective-permute-start | bytes 294920 | tf_op jit(solution)/shard_map/ppermute | solution.py:336
  119.8 10.9 %collective-permute-start.13 = (f32[2,2,96,64]{3,2,0,1:T(8,128)S(1)}, f32[2,2,96,64]{3,2,0,1:T(8,128)S(1)}, u32[]{:S(2)}, u32[]{:S(2)}) collective-permute-start(f32[2,2,96,64]{3,2,0,1:T(8,128)S(1)} %get-tuple-element.39), channel_id=1, source_target_pairs={{4,0},{8,4},{12,8},{16,12},{20,16},{24,20},{28,24},{5,1},{9,5},{13... | collective-permute-start | bytes 294920 | tf_op jit(solution)/shard_map/ppermute | solution.py:337
